TPU v7x, 32 devices: a whole 2x2x4 slice. The times are simulated.
32 devices in a mesh: seg: 8 (over z, core), bond: 4 (over y, x).
Axes of the slice: x: 2, y: 2, z: 4, core: 2. Of those that a mesh axis runs over, the one named last changes fastest.
Arguments:
- left_env: bfloat16 [8, 1024, 6, 1024], P('seg', 'bond'), may hold values from -0.1875 to 0.1875
- prev_left: bfloat16 [8, 1024, 1024], P('seg'), may hold values from -0.25 to 1.25
- cur_site: bfloat16 [8, 1024, 4, 1024], P('seg', 'bond'), may hold values from -6 to 6
- prev_site: bfloat16 [8, 1024, 4, 1024], P('seg', None, None, 'bond'), may hold values from -6 to 6
- hamiltonian: bfloat16 [8, 6, 6, 4, 4], P('seg'), may hold values from -1.25 to 1.25
- right_env: bfloat16 [8, 1024, 6, 1024], P('seg', 'bond'), may hold values from -0.078125 to 0.078125
- prev_right: bfloat16 [8, 1024, 1024], P('seg'), may hold values from -0.25 to 1.25
Outputs:
- new_site: bfloat16 [8, 1024, 4, 1024], P('seg', 'bond')
- center: float32 [8, 1024, 1024], P('seg', 'bond')
All inputs are finite; a program needn't handle non-finite values.
Results may differ from a plain program's by a relative error of at most 0.0054.
Values may be sent and summed in bfloat16 or wider, within the bound.
A program may use at most 128 MiB of HBM per device.

v0:
```python
import math
import jax
import jax.numpy as jnp
from jax import lax
from jax.sharding import PartitionSpec as P

PHYS = 4
MPOB = 6


def shifted(block, axis, distance):
    devices = range(lax.axis_size(axis))
    route = [((i - distance) % len(devices), i) for i in devices]
    return lax.ppermute(block, axis, route)


def shards(left_env, prev_left, cur_site, prev_site, hamiltonian, right_env, prev_right):
    left_now, prev_now = shifted((left_env[0], prev_left[0]), "seg", 1)
    own_rows = left_now.shape[0]
    bond_width = left_now.shape[2]
    coupling = hamiltonian[0].astype(jnp.float32)
    current = lax.all_gather(cur_site[0], "bond", axis=0, tiled=True)
    projected = jnp.dot(
        left_now.reshape(own_rows * MPOB, bond_width),
        current.reshape(bond_width, PHYS * bond_width),
        preferred_element_type=jnp.float32,
    ).reshape(own_rows, MPOB, PHYS, bond_width)
    mixture = jnp.einsum(
        "autc,uvst->asvc", projected, coupling, precision=lax.Precision.HIGHEST
    ).astype(jnp.bfloat16)
    applied = jnp.einsum(
        "asvc,cvy->asy",
        mixture,
        lax.all_gather(right_env[0], "bond", axis=0, tiled=True),
        preferred_element_type=jnp.float32,
    )
    partial_value = jnp.einsum(
        "ab,bsc->asc", prev_now, prev_site[0], preferred_element_type=jnp.float32
    ).astype(jnp.bfloat16)
    second = jnp.einsum(
        "akc,cy->aky",
        lax.all_to_all(partial_value, "bond", split_axis=0, concat_axis=2, tiled=True),
        prev_right[0],
        preferred_element_type=jnp.float32,
    )
    target = (2.0 * applied - second).reshape(own_rows * PHYS, bond_width)
    local_correlation = jnp.dot(
        target.T, target, precision=lax.Precision.HIGHEST, preferred_element_type=jnp.float32
    )
    correlation = lax.psum(local_correlation, "bond")
    triangle = jnp.linalg.cholesky(correlation)
    solved = jax.scipy.linalg.solve_triangular(triangle, target.T, lower=True)
    norming = math.sqrt(bond_width * PHYS)
    new_site = (solved.T * norming).astype(jnp.bfloat16).reshape(1, own_rows, PHYS, bond_width)
    offset = lax.axis_index("bond") * own_rows
    center = lax.dynamic_slice_in_dim(triangle.T, offset, own_rows, 0) / norming
    return (new_site, center[None])


def solution(mesh):
    return jax.shard_map(
        shards,
        mesh=mesh,
        in_specs=(
            P("seg", "bond", None, None),
            P("seg", None, None),
            P("seg", "bond", None, None),
            P("seg", None, None, "bond"),
            P("seg", None, None, None, None),
            P("seg", "bond", None, None),
            P("seg", None, None),
        ),
        out_specs=(P("seg", "bond", None, None), P("seg", "bond", None)),
        check_vma=False,
    )
```

profile of v0, /device:TPU:0, one launch (start us, length us, event | category | flops | bytes accessed | tf_op | source)
XLA Modules:
  0.0 759.1 jit_solution(3926485406650583413)
XLA Ops:
  9.3 2.7 collective-permute-start
  11.9 25.3 %collective-permute-done.1 = bf16[1024,1024]{1,0:T(8,128)(2,1)S(1)} collective-permute-done((bf16[1024,1024]{1,0:T(8,128)(2,1)}, bf16[1024,1024]{1,0:T(8,128)(2,1)S(1)}, u32[]{:S(2)}, u32[]{:S(2)}) %collective-permute-start.1) | collective-permute-done | bytes 2097184 | tf_op jit(solution)/shard_map/ppermute | solution.py:14
  37.2 2.3 fusion.31
  41.2 40.1 %all_to_all.18 = bf16[1024,4,256]{2,1,0:T(4,128)(2,1)S(1)} all-to-all(bf16[1024,4,256]{2,1,0:T(4,128)(2,1)S(1)} %copy.30), channel_id=1, replica_groups=mesh['seg'=8,'bond'=4] {'bond'}, dimensions={0} | all-to-all | bytes 4194304 | tf_op jit(solution)/shard_map/all_to_all | solution.py:42
  82.9 2.7 all_to_all.16
  85.6 6.5 fusion.26
  92.1 22.9 %all-gather.5.cloned.1.call-done = bf16[1,1024,4,1024]{3,2,0,1:T(4,128)(2,1)} async-done(((bf16[1,256,4,1024]{3,2,0,1:T(4,128)(2,1)}), bf16[1,1024,4,1024]{3,2,0,1:T(4,128)(2,1)}) %all-gather.5.cloned.1.call-update) | async-done | bytes 8388624 | tf_op jit(solution)/shard_map/all_gather | solution.py:22
  115.0 14.1 %copy.45 = bf16[1,1024,4,1024]{1,3,2,0:T(8,128)(2,1)} copy(bf16[1,1024,4,1024]{3,2,0,1:T(4,128)(2,1)} %all-gather.5.cloned.1.call-done) | data formatting | bytes 16777216 | tf_op jit(solution)/shard_map/reshape | solution.py:25
  129.1 21.9 %convolution_bitcast_fusion = f32[256,6,4,1024,1]{3,0,2,1,4:T(8,128)} fusion(bf16[1,1024,4,1024]{1,3,2,0:T(8,128)(2,1)} %copy.45, bf16[256,6,1024]{2,0,1:T(8,128)(2,1)} %collective-permute-done), kind=kOutput, calls=%fused_computation.9 | convolution fusion | flops 12884901888 | bytes 36700160 | tf_op jit(solution)/shard_map/dot_general | solution.py:23
  151.0 62.8 %fusion.2 = bf16[256,4,6,1024]{3,2,1,0:T(8,128)(2,1)} fusion(f32[256,6,4,1024,1]{3,0,2,1,4:T(8,128)} %convolution_bitcast_fusion, bf16[1,6,6,4,4]{2,4,3,1,0:T(4,128)(2,1)S(1)} %copy-done.5), kind=kOutput, calls=%fused_computation.5 | convolution fusion | flops 1818230784 | bytes 37749888 | tf_op jit(solution)/shard_map/autc,uvst->asvc/dot_general | solution.py:28
  213.7 25.5 %all-gather.7.cloned.1.call-done = bf16[1,1024,6,1024]{3,1,2,0:T(8,128)(2,1)} async-done(((bf16[1,256,6,1024]{3,1,2,0:T(8,128)(2,1)}), bf16[1,1024,6,1024]{3,1,2,0:T(8,128)(2,1)}) %all-gather.7.cloned.1.call-update) | async-done | bytes 12582928 | tf_op jit(solution)/shard_map/all_gather | solution.py:34
  239.2 32.4 %fusion.10 = f32[256,4,1024]{2,0,1:T(8,128)S(1)} fusion(f32[256,4,1024]{2,0,1:T(8,128)} %fusion.26, bf16[1,1024,6,1024]{3,1,2,0:T(8,128)(2,1)} %all-gather.7.cloned.1.call-done, bf16[256,4,6,1024]{3,2,1,0:T(8,128)(2,1)} %fusion.2), kind=kOutput, calls=%fused_computation.14 | convolution fusion | flops 12886999040 | bytes 33554432 | tf_op jit(solution)/shard_map/asvc,cvy->asy/dot_general | solution.py:31
  271.7 1.9 copy-done.4
  273.6 15.1 %convolution_bitcast_fusion.1 = f32[1024,1024]{0,1:T(8,128)} fusion(f32[256,4,1024]{2,0,1:T(8,128)S(1)} %fusion.10), kind=kOutput, calls=%fused_computation.20 | convolution fusion | flops 12884901888 | bytes 8388608 | tf_op jit(solution)/shard_map/dot_general | solution.py:47
  288.8 6.8 copy.35
  295.6 5.3 reshape.94
  300.9 5.5 copy.36
  306.4 86.1 %all-reduce.3.cloned.1.call-done = f32[1024,1024]{0,1:T(8,128)} async-done(((f32[1024,1024]{0,1:T(8,128)}), f32[1024,1024]{0,1:T(8,128)}) %all-reduce.3.cloned.1.call-update) | async-done | bytes 4194320 | tf_op jit(solution)/shard_map/psum | solution.py:50
  392.5 5.7 copy.34
  398.3 4.4 fusion.9
  402.7 2.0 copy-done.3
  404.7 11.7 %cholesky.223 = f32[128,128]{1,0:T(8,128)S(1)} custom-call(f32[128,128]{1,0:T(8,128)S(1)} %cholesky.580), custom_call_target="Cholesky" | custom-call | tf_op jit(solution)/shard_map/jit(cholesky)/cholesky | solution.py:51
  416.4 9.8 %custom-call.63 = f32[1,128,128]{1,2,0:T(8,128)S(1)} custom-call(f32[1,128,128]{2,1,0:T(8,128)S(1)} %get-tuple-element.74), custom_call_target="InvertDiagBlocksLowerTriangular" | custom-call | tf_op jit(solution)/shard_map/jit(cholesky)/cholesky | solution.py:51
  426.3 2.5 cholesky.255
  428.7 2.4 constant_dynamic-update-slice_fusion.32
  432.7 11.9 %cholesky.244 = f32[128,128]{1,0:T(8,128)S(1)} custom-call(f32[128,128]{1,0:T(8,128)S(1)} %cholesky.584), custom_call_target="Cholesky" | custom-call | tf_op jit(solution)/shard_map/jit(cholesky)/cholesky | solution.py:51
  445.2 9.8 %custom-call.64 = f32[1,128,128]{1,2,0:T(8,128)S(1)} custom-call(f32[1,128,128]{2,1,0:T(8,128)S(1)} %get-tuple-element.71), custom_call_target="InvertDiagBlocksLowerTriangular" | custom-call | tf_op jit(solution)/shard_map/jit(cholesky)/cholesky | solution.py:51
  456.3 2.1 convolution_subtract_fusion.6
  458.4 11.7 %cholesky.468 = f32[128,128]{1,0:T(8,128)S(1)} custom-call(f32[128,128]{1,0:T(8,128)S(1)} %cholesky.589), custom_call_target="Cholesky" | custom-call | tf_op jit(solution)/shard_map/jit(cholesky)/cholesky | solution.py:51
  471.4 9.8 %custom-call.65 = f32[1,128,128]{1,2,0:T(8,128)S(1)} custom-call(f32[1,128,128]{2,1,0:T(8,128)S(1)} %get-tuple-element.68), custom_call_target="InvertDiagBlocksLowerTriangular" | custom-call | tf_op jit(solution)/shard_map/jit(cholesky)/cholesky | solution.py:51
  482.4 2.3 convolution_subtract_fusion.7
  484.7 11.9 %cholesky.487 = f32[128,128]{1,0:T(8,128)S(1)} custom-call(f32[128,128]{1,0:T(8,128)S(1)} %cholesky.594), custom_call_target="Cholesky" | custom-call | tf_op jit(solution)/shard_map/jit(cholesky)/cholesky | solution.py:51
  497.9 9.8 %custom-call.66 = f32[1,128,128]{1,2,0:T(8,128)S(1)} custom-call(f32[1,128,128]{2,1,0:T(8,128)S(1)} %get-tuple-element.65), custom_call_target="InvertDiagBlocksLowerTriangular" | custom-call | tf_op jit(solution)/shard_map/jit(cholesky)/cholesky | solution.py:51
  508.8 2.3 convolution_subtract_fusion.8
  511.2 11.7 %cholesky.506 = f32[128,128]{1,0:T(8,128)S(1)} custom-call(f32[128,128]{1,0:T(8,128)S(1)} %cholesky.599), custom_call_target="Cholesky" | custom-call | tf_op jit(solution)/shard_map/jit(cholesky)/cholesky | solution.py:51
  524.2 10.2 %custom-call.67 = f32[1,128,128]{1,2,0:T(8,128)S(1)} custom-call(f32[1,128,128]{2,1,0:T(8,128)S(1)} %get-tuple-element.62), custom_call_target="InvertDiagBlocksLowerTriangular" | custom-call | tf_op jit(solution)/shard_map/jit(cholesky)/cholesky | solution.py:51
  535.4 2.3 convolution_subtract_fusion.9
  537.7 11.7 %cholesky.526 = f32[128,128]{1,0:T(8,128)S(1)} custom-call(f32[128,128]{1,0:T(8,128)S(1)} %cholesky.604), custom_call_target="Cholesky" | custom-call | tf_op jit(solution)/shard_map/jit(cholesky)/cholesky | solution.py:51
  550.7 9.8 %custom-call.68 = f32[1,128,128]{1,2,0:T(8,128)S(1)} custom-call(f32[1,128,128]{2,1,0:T(8,128)S(1)} %get-tuple-element.59), custom_call_target="InvertDiagBlocksLowerTriangular" | custom-call | tf_op jit(solution)/shard_map/jit(cholesky)/cholesky | solution.py:51
  561.4 2.0 convolution_subtract_fusion.10
  563.5 11.9 %cholesky.546 = f32[128,128]{1,0:T(8,128)S(1)} custom-call(f32[128,128]{1,0:T(8,128)S(1)} %cholesky.609), custom_call_target="Cholesky" | custom-call | tf_op jit(solution)/shard_map/jit(cholesky)/cholesky | solution.py:51
  576.6 9.8 %custom-call.69 = f32[1,128,128]{1,2,0:T(8,128)S(1)} custom-call(f32[1,128,128]{2,1,0:T(8,128)S(1)} %get-tuple-element.56), custom_call_target="InvertDiagBlocksLowerTriangular" | custom-call | tf_op jit(solution)/shard_map/jit(cholesky)/cholesky | solution.py:51
  587.2 1.8 convolution_subtract_fusion.11
  589.0 11.7 %cholesky.564 = f32[128,128]{1,0:T(8,128)S(1)} custom-call(f32[128,128]{1,0:T(8,128)S(1)} %convolution_subtract_fusion.11), custom_call_target="Cholesky" | custom-call | tf_op jit(solution)/shard_map/jit(cholesky)/cholesky | solution.py:51
  607.6 6.7 fusion.11
  614.3 23.0 %while.1 = (s32[]{:T(128)}, f32[1024,1024]{1,0:T(8,128)}, s32[8,2]{0,1:T(2,128)S(1)}, f32[8,128,128]{2,1,0:T(8,128)S(1)}, s32[]{:T(128)}) while((s32[]{:T(128)}, f32[1024,1024]{1,0:T(8,128)}, s32[8,2]{0,1:T(2,128)S(1)}, f32[8,128,128]{2,1,0:T(8,128)S(1)}, s32[]{:T(128)}) %tuple.65), condition=%wide.while_cond, body=%wide.while_body.sunk | while | flops 2 | bytes 131181 | solution.py:52
  614.9 2.3 bitcast_dynamic-update-slice_fusion.2
  617.8 2.3 bitcast_dynamic-update-slice_fusion.2
  620.7 2.3 bitcast_dynamic-update-slice_fusion.2
  623.6 2.3 bitcast_dynamic-update-slice_fusion.2
  626.5 2.3 bitcast_dynamic-update-slice_fusion.2
  629.4 2.3 bitcast_dynamic-update-slice_fusion.2
  632.3 2.3 bitcast_dynamic-update-slice_fusion.2
  635.1 2.2 bitcast_dynamic-update-slice_fusion.2
  637.3 78.8 %custom-call.70 = f32[8,128,128]{1,2,0:T(8,128)S(1)} custom-call(f32[8,128,128]{2,1,0:T(8,128)S(1)} %get-tuple-element.9), custom_call_target="InvertDiagBlocksLowerTriangular" | custom-call | tf_op jit(solution)/shard_map/jit(_solve_triangular)/triangular_solve | solution.py:52
  716.2 1.9 constant_dynamic-update-slice_fusion.17
  722.9 2.0 fusion.42
  725.7 2.2 fusion.45
  728.6 2.6 convolution_subtract_fusion.2
  732.0 2.8 convolution_subtract_fusion.1
  735.4 3.5 convolution_subtract_fusion.3
  739.6 1.9 fusion.17
  741.5 4.1 copy.37
  745.6 4.1 reshape.95
  (79 shorter events, 38.0 us)
Async XLA Ops:
  7.2 30.0 %copy-start = (bf16[1,1024,4,256]{3,2,1,0:T(4,128)(2,1)S(1)}, bf16[1,1024,4,256]{3,2,1,0:T(4,128)(2,1)}, u32[]{:S(2)}) copy-start(bf16[1,1024,4,256]{3,2,1,0:T(4,128)(2,1)} %param.10) | copy-start | bytes 6291460
  7.2 107.8 %all-gather.5.cloned.1.call-start = ((), (), s32[]{:S(2)}) async-start(), calls=%async_computation.2 | async-start | bytes 10485760 | tf_op jit(solution)/shard_map/all_gather | solution.py:22
  7.9 231.3 %all-gather.7.cloned.1.call-start = ((), (), s32[]{:S(2)}) async-start(), calls=%async_computation.3 | async-start | bytes 15728640 | tf_op jit(solution)/shard_map/all_gather | solution.py:34
  8.7 383.9 %all-reduce.3.cloned.1.call-start = ((), (), s32[]{:S(2)}) async-start(), calls=%async_computation.1 | async-start | bytes 8388608 | tf_op jit(solution)/shard_map/psum | solution.py:50
  8.7 28.5 %collective-permute-start.1 = (bf16[1024,1024]{1,0:T(8,128)(2,1)}, bf16[1024,1024]{1,0:T(8,128)(2,1)S(1)}, u32[]{:S(2)}, u32[]{:S(2)}) collective-permute-start(bf16[1024,1024]{1,0:T(8,128)(2,1)} %bitcast.186), channel_id=1, source_target_pairs={{28,0},{0,4},{4,8},{8,12},{12,16},{16,20},{20,24},{24,28},{29,1},{... | collective-permute-start | bytes 6291464 | tf_op jit(solution)/shard_map/ppermute | solution.py:14
  9.3 119.9 %collective-permute-start = (bf16[256,6,1024]{2,0,1:T(8,128)(2,1)}, bf16[256,6,1024]{2,0,1:T(8,128)(2,1)}, u32[]{:S(2)}, u32[]{:S(2)}) collective-permute-start(bf16[256,6,1024]{2,0,1:T(8,128)(2,1)} %bitcast.185), channel_id=1, source_target_pairs={{28,0},{0,4},{4,8},{8,12},{12,16},{16,20},{20,24},{24,28},{29,1},{... | collective-permute-start | bytes 9437192 | tf_op jit(solution)/shard_map/ppermute | solution.py:14
  129.1 21.9 %copy-start.5 = (bf16[1,6,6,4,4]{2,4,3,1,0:T(4,128)(2,1)S(1)}, bf16[1,6,6,4,4]{2,4,3,1,0:T(4,128)(2,1)}, u32[]{:S(2)}) copy-start(bf16[1,6,6,4,4]{2,4,3,1,0:T(4,128)(2,1)} %param.11) | copy-start | bytes 3460
  271.7 1.9 copy-start.4
  402.7 2.0 copy-start.3
  716.2 4.3 copy-start.2
  741.5 10.8 %copy-start.1 = (bf16[1,1024,4,256]{3,2,1,0:T(4,128)(2,1)S(1)}, bf16[1,1024,4,256]{3,2,1,0:T(4,128)(2,1)}, u32[]{:S(2)}) copy-start(bf16[1,1024,4,256]{3,2,1,0:T(4,128)(2,1)} %param.10) | copy-start | bytes 6291460
Sparse Core Ops, SparseCore 0:
  9.8 105.0 all-gather.4
  116.8 122.3 all-gather.6
  288.9 103.5 all-reduce.2
where the time goes:
time: 764 us; the launch traced here: 759 us
  other arithmetic  265 us (35%)
  matrix products  187 us (24%)
  waiting for transfers between devices  161 us (21%)
  local copies, waits for them, and re-layouts  82.3 us (11%)
  blocking collectives  40.1 us (5%)
  between operations  19.3 us (3%)
    another operation x30, other arithmetic, shards(): triangle = jnp.linalg.cholesky(correlation)  172 us
    psum x1, waiting for transfers between devices, shards(): correlation = lax.psum(local_correlation, 'bond')  86.1 us
    another operation x3, other arithmetic, shards(): solved = jax.scipy.linalg.solve_triangular(triangle, target.T, lower=True)  85.5 us
    dot_general x1, matrix products, shards(): jnp.einsum('autc,uvst->asvc', projected, coupling, precision=lax.Precisio...  62.8 us
    all_to_all x1, blocking collectives, shards(): lax.all_to_all(partial_value, 'bond', split_axis=0, concat_axis=2, tiled=...  40.1 us
    dot_general x1, matrix products, shards(): jnp.einsum('asvc,cvy->asy', mixture, lax.all_gather(right_env[0], 'bond',...  32.4 us
    all_gather x1, waiting for transfers between devices, shards(): lax.all_gather(right_env[0], 'bond', axis=0, tiled=True)  25.5 us
    ppermute x2, waiting for transfers between devices, shifted(): return lax.ppermute(block, axis, route)  25.3 us
  transfers between devices with their start and end apart: 5, of which 4 were waited for; matrix products, arithmetic and copies ran while one was open for 17% of the time, Pallas kernels for 0%

commit v1 on v0

--- a/solution.py
+++ b/solution.py
@@ -1,3 +1,4 @@
+import functools
 import math
 import jax
 import jax.numpy as jnp
@@ -6,6 +7,25 @@
 
 PHYS = 4
 MPOB = 6
+
+
+def _order_vector(message, lane_axis):
+    nd = lax.axis_size(lane_axis)
+
+    def order_ranges(taken_in, finding):
+        if finding >= nd:
+            return taken_in
+        y_new = order_ranges(
+            taken_in + lax.ppermute(taken_in, lane_axis, [(dd, dd ^ finding) for dd in range(nd)]),
+            2 * finding,
+        )
+        return y_new
+
+    top = order_ranges(message, 1)
+    return top
+
+
+assign_skins = functools.partial(_order_vector, lane_axis="bond")
 
 
 def shifted(block, axis, distance):
@@ -47,7 +67,7 @@
     local_correlation = jnp.dot(
         target.T, target, precision=lax.Precision.HIGHEST, preferred_element_type=jnp.float32
     )
-    correlation = lax.psum(local_correlation, "bond")
+    correlation = assign_skins(local_correlation)
     triangle = jnp.linalg.cholesky(correlation)
     solved = jax.scipy.linalg.solve_triangular(triangle, target.T, lower=True)
     norming = math.sqrt(bond_width * PHYS)

time: 764 us -> 852 us (1.12)
  waiting for transfers between devices: 161 us -> 238 us
  other arithmetic: 265 us -> 275 us
    ppermute x0 -> x2, waiting for transfers between devices: none -> 163 us  [order_ranges(): lax.ppermute(taken_in, lane_axis, [(dd, dd ^ finding) for dd in range(nd)])]
    psum x1 -> x0, waiting for transfers between devices: 86.1 us -> none  [shards(): correlation = lax.psum(local_correlation, 'bond')]
    add x0 -> x2, other arithmetic: none -> 9.71 us  [order_ranges(): taken_in + lax.ppermute(taken_in, lane_axis, [(dd, dd ^ finding) for dd i...]
  transfers between devices with their start and end apart: 5 -> 6, of which waited for: 4 -> 5; matrix products, arithmetic and copies ran while one was open for 17% -> 15% of each run, Pallas kernels for 0% -> 0%
where the time goes in v1:
time: 852 us; the launch traced here: 847 us
  other arithmetic  275 us (32%)
  waiting for transfers between devices  238 us (28%)
  matrix products  187 us (22%)
  local copies, waits for them, and re-layouts  80 us (9%)
  blocking collectives  40.4 us (5%)
  between operations  19.5 us (2%)
    another operation x30, other arithmetic, shards(): triangle = jnp.linalg.cholesky(correlation)  172 us
    ppermute x2, waiting for transfers between devices, order_ranges(): lax.ppermute(taken_in, lane_axis, [(dd, dd ^ finding) for dd in range(nd)])  163 us
    another operation x3, other arithmetic, shards(): solved = jax.scipy.linalg.solve_triangular(triangle, target.T, lower=True)  85.7 us
    dot_general x1, matrix products, shards(): jnp.einsum('autc,uvst->asvc', projected, coupling, precision=lax.Precisio...  62.9 us
    all_to_all x1, blocking collectives, shards(): lax.all_to_all(partial_value, 'bond', split_axis=0, concat_axis=2, tiled=...  40.4 us
    dot_general x1, matrix products, shards(): jnp.einsum('asvc,cvy->asy', mixture, lax.all_gather(right_env[0], 'bond',...  32.4 us
    all_gather x1, waiting for transfers between devices, shards(): lax.all_gather(right_env[0], 'bond', axis=0, tiled=True)  25.3 us
    ppermute x2, waiting for transfers between devices, shifted(): return lax.ppermute(block, axis, route)  25.3 us
  transfers between devices with their start and end apart: 6, of which 5 were waited for; matrix products, arithmetic and copies ran while one was open for 15% of the time, Pallas kernels for 0%

profile of v1, /device:TPU:0, one launch (start us, length us, event | category | flops | bytes accessed | tf_op | source)
XLA Modules:
  0.0 846.8 jit_solution(2606033033993808745)
XLA Ops:
  9.2 2.7 collective-permute-start
  11.9 25.3 %collective-permute-done.1 = bf16[1024,1024]{1,0:T(8,128)(2,1)S(1)} collective-permute-done((bf16[1024,1024]{1,0:T(8,128)(2,1)}, bf16[1024,1024]{1,0:T(8,128)(2,1)S(1)}, u32[]{:S(2)}, u32[]{:S(2)}) %collective-permute-start.1) | collective-permute-done | bytes 2097184 | tf_op jit(solution)/shard_map/ppermute | solution.py:34
  37.2 2.3 fusion.31
  41.1 40.4 %all_to_all.18 = bf16[1024,4,256]{2,1,0:T(4,128)(2,1)S(1)} all-to-all(bf16[1024,4,256]{2,1,0:T(4,128)(2,1)S(1)} %copy.32), channel_id=1, replica_groups=mesh['seg'=8,'bond'=4] {'bond'}, dimensions={0} | all-to-all | bytes 4194304 | tf_op jit(solution)/shard_map/all_to_all | solution.py:62
  83.1 2.7 all_to_all.16
  85.8 6.5 fusion.26
  92.3 22.6 %all-gather.5.cloned.1.call-done = bf16[1,1024,4,1024]{3,2,0,1:T(4,128)(2,1)} async-done(((bf16[1,256,4,1024]{3,2,0,1:T(4,128)(2,1)}), bf16[1,1024,4,1024]{3,2,0,1:T(4,128)(2,1)}) %all-gather.5.cloned.1.call-update) | async-done | bytes 8388624 | tf_op jit(solution)/shard_map/all_gather | solution.py:42
  115.0 14.1 %copy.48 = bf16[1,1024,4,1024]{1,3,2,0:T(8,128)(2,1)} copy(bf16[1,1024,4,1024]{3,2,0,1:T(4,128)(2,1)} %all-gather.5.cloned.1.call-done) | data formatting | bytes 16777216 | tf_op jit(solution)/shard_map/reshape | solution.py:45
  129.1 21.9 %convolution_bitcast_fusion = f32[256,6,4,1024,1]{3,0,2,1,4:T(8,128)} fusion(bf16[1,1024,4,1024]{1,3,2,0:T(8,128)(2,1)} %copy.48, bf16[256,6,1024]{2,0,1:T(8,128)(2,1)} %collective-permute-done), kind=kOutput, calls=%fused_computation.9 | convolution fusion | flops 12884901888 | bytes 36700160 | tf_op jit(solution)/shard_map/dot_general | solution.py:43
  151.0 62.9 %fusion.2 = bf16[256,4,6,1024]{3,2,1,0:T(8,128)(2,1)} fusion(f32[256,6,4,1024,1]{3,0,2,1,4:T(8,128)} %convolution_bitcast_fusion, bf16[1,6,6,4,4]{2,4,3,1,0:T(4,128)(2,1)S(1)} %copy-done.5), kind=kOutput, calls=%fused_computation.5 | convolution fusion | flops 1818230784 | bytes 37749888 | tf_op jit(solution)/shard_map/autc,uvst->asvc/dot_general | solution.py:48
  213.9 25.3 %all-gather.7.cloned.1.call-done = bf16[1,1024,6,1024]{3,1,2,0:T(8,128)(2,1)} async-done(((bf16[1,256,6,1024]{3,1,2,0:T(8,128)(2,1)}), bf16[1,1024,6,1024]{3,1,2,0:T(8,128)(2,1)}) %all-gather.7.cloned.1.call-update) | async-done | bytes 12582928 | tf_op jit(solution)/shard_map/all_gather | solution.py:54
  239.2 32.4 %fusion.10 = f32[256,4,1024]{2,0,1:T(8,128)S(1)} fusion(f32[256,4,1024]{2,0,1:T(8,128)} %fusion.26, bf16[1,1024,6,1024]{3,1,2,0:T(8,128)(2,1)} %all-gather.7.cloned.1.call-done, bf16[256,4,6,1024]{3,2,1,0:T(8,128)(2,1)} %fusion.2), kind=kOutput, calls=%fused_computation.14 | convolution fusion | flops 12886999040 | bytes 33554432 | tf_op jit(solution)/shard_map/asvc,cvy->asy/dot_general | solution.py:51
  271.7 14.8 %convolution_bitcast_fusion.1 = f32[1024,1024]{0,1:T(8,128)S(1)} fusion(f32[256,4,1024]{2,0,1:T(8,128)S(1)} %fusion.10), kind=kOutput, calls=%fused_computation.20 | convolution fusion | flops 12884901888 | bytes 8388608 | tf_op jit(solution)/shard_map/dot_general | solution.py:67
  288.1 90.7 %collective-permute-done.2 = f32[1024,1024]{0,1:T(8,128)S(1)} collective-permute-done((f32[1024,1024]{0,1:T(8,128)S(1)}, f32[1024,1024]{0,1:T(8,128)S(1)}, u32[]{:S(2)}, u32[]{:S(2)}) %collective-permute-start.2) | collective-permute-done | bytes 4194336 | tf_op jit(solution)/shard_map/ppermute | solution.py:19
  378.8 2.9 add.86
  383.1 6.8 copy.38
  390.0 5.3 reshape.94
  395.3 5.3 copy.39
  400.6 72.7 %collective-permute-done.3 = f32[1024,1024]{0,1:T(8,128)} collective-permute-done((f32[1024,1024]{0,1:T(8,128)}, f32[1024,1024]{0,1:T(8,128)}, u32[]{:S(2)}, u32[]{:S(2)}) %collective-permute-start.3) | collective-permute-done | bytes 4194336 | tf_op jit(solution)/shard_map/ppermute | solution.py:19
  473.3 6.8 add.87
  480.1 5.5 copy.37
  485.6 4.4 fusion.9
  490.0 2.0 copy-done.3
  492.0 11.7 %cholesky.223 = f32[128,128]{1,0:T(8,128)S(1)} custom-call(f32[128,128]{1,0:T(8,128)S(1)} %cholesky.580), custom_call_target="Cholesky" | custom-call | tf_op jit(solution)/shard_map/jit(cholesky)/cholesky | solution.py:71
  503.7 9.8 %custom-call.63 = f32[1,128,128]{1,2,0:T(8,128)S(1)} custom-call(f32[1,128,128]{2,1,0:T(8,128)S(1)} %get-tuple-element.74), custom_call_target="InvertDiagBlocksLowerTriangular" | custom-call | tf_op jit(solution)/shard_map/jit(cholesky)/cholesky | solution.py:71
  513.6 2.5 cholesky.255
  516.0 2.4 constant_dynamic-update-slice_fusion.32
  520.0 11.9 %cholesky.244 = f32[128,128]{1,0:T(8,128)S(1)} custom-call(f32[128,128]{1,0:T(8,128)S(1)} %cholesky.584), custom_call_target="Cholesky" | custom-call | tf_op jit(solution)/shard_map/jit(cholesky)/cholesky | solution.py:71
  532.6 9.8 %custom-call.64 = f32[1,128,128]{1,2,0:T(8,128)S(1)} custom-call(f32[1,128,128]{2,1,0:T(8,128)S(1)} %get-tuple-element.71), custom_call_target="InvertDiagBlocksLowerTriangular" | custom-call | tf_op jit(solution)/shard_map/jit(cholesky)/cholesky | solution.py:71
  543.6 2.1 slice_subtract_fusion.1
  545.7 11.7 %cholesky.468 = f32[128,128]{1,0:T(8,128)S(1)} custom-call(f32[128,128]{1,0:T(8,128)S(1)} %cholesky.589), custom_call_target="Cholesky" | custom-call | tf_op jit(solution)/shard_map/jit(cholesky)/cholesky | solution.py:71
  558.7 9.8 %custom-call.65 = f32[1,128,128]{1,2,0:T(8,128)S(1)} custom-call(f32[1,128,128]{2,1,0:T(8,128)S(1)} %get-tuple-element.68), custom_call_target="InvertDiagBlocksLowerTriangular" | custom-call | tf_op jit(solution)/shard_map/jit(cholesky)/cholesky | solution.py:71
  569.7 2.3 slice_subtract_fusion.2
  572.0 12.1 %cholesky.487 = f32[128,128]{1,0:T(8,128)S(1)} custom-call(f32[128,128]{1,0:T(8,128)S(1)} %cholesky.594), custom_call_target="Cholesky" | custom-call | tf_op jit(solution)/shard_map/jit(cholesky)/cholesky | solution.py:71
  585.4 9.8 %custom-call.66 = f32[1,128,128]{1,2,0:T(8,128)S(1)} custom-call(f32[1,128,128]{2,1,0:T(8,128)S(1)} %get-tuple-element.65), custom_call_target="InvertDiagBlocksLowerTriangular" | custom-call | tf_op jit(solution)/shard_map/jit(cholesky)/cholesky | solution.py:71
  596.3 2.3 slice_subtract_fusion.3
  598.7 11.7 %cholesky.506 = f32[128,128]{1,0:T(8,128)S(1)} custom-call(f32[128,128]{1,0:T(8,128)S(1)} %cholesky.599), custom_call_target="Cholesky" | custom-call | tf_op jit(solution)/shard_map/jit(cholesky)/cholesky | solution.py:71
  611.7 9.9 %custom-call.67 = f32[1,128,128]{1,2,0:T(8,128)S(1)} custom-call(f32[1,128,128]{2,1,0:T(8,128)S(1)} %get-tuple-element.62), custom_call_target="InvertDiagBlocksLowerTriangular" | custom-call | tf_op jit(solution)/shard_map/jit(cholesky)/cholesky | solution.py:71
  622.7 2.3 slice_subtract_fusion.4
  625.0 11.7 %cholesky.526 = f32[128,128]{1,0:T(8,128)S(1)} custom-call(f32[128,128]{1,0:T(8,128)S(1)} %cholesky.604), custom_call_target="Cholesky" | custom-call | tf_op jit(solution)/shard_map/jit(cholesky)/cholesky | solution.py:71
  638.0 9.8 %custom-call.68 = f32[1,128,128]{1,2,0:T(8,128)S(1)} custom-call(f32[1,128,128]{2,1,0:T(8,128)S(1)} %get-tuple-element.59), custom_call_target="InvertDiagBlocksLowerTriangular" | custom-call | tf_op jit(solution)/shard_map/jit(cholesky)/cholesky | solution.py:71
  648.7 2.0 slice_subtract_fusion.5
  650.8 11.9 %cholesky.546 = f32[128,128]{1,0:T(8,128)S(1)} custom-call(f32[128,128]{1,0:T(8,128)S(1)} %cholesky.609), custom_call_target="Cholesky" | custom-call | tf_op jit(solution)/shard_map/jit(cholesky)/cholesky | solution.py:71
  663.9 9.8 %custom-call.69 = f32[1,128,128]{1,2,0:T(8,128)S(1)} custom-call(f32[1,128,128]{2,1,0:T(8,128)S(1)} %get-tuple-element.56), custom_call_target="InvertDiagBlocksLowerTriangular" | custom-call | tf_op jit(solution)/shard_map/jit(cholesky)/cholesky | solution.py:71
  676.3 11.7 %cholesky.564 = f32[128,128]{1,0:T(8,128)S(1)} custom-call(f32[128,128]{1,0:T(8,128)S(1)} %slice_subtract_fusion.6), custom_call_target="Cholesky" | custom-call | tf_op jit(solution)/shard_map/jit(cholesky)/cholesky | solution.py:71
  695.0 6.7 fusion.11
  701.6 23.0 %while.1 = (s32[]{:T(128)}, f32[1024,1024]{1,0:T(8,128)}, s32[8,2]{0,1:T(2,128)S(1)}, f32[8,128,128]{2,1,0:T(8,128)S(1)}, s32[]{:T(128)}) while((s32[]{:T(128)}, f32[1024,1024]{1,0:T(8,128)}, s32[8,2]{0,1:T(2,128)S(1)}, f32[8,128,128]{2,1,0:T(8,128)S(1)}, s32[]{:T(128)}) %tuple.65), condition=%wide.while_cond, body=%wide.while_body.sunk | while | flops 2 | bytes 131181 | solution.py:72
  702.2 2.3 bitcast_dynamic-update-slice_fusion.2
  705.1 2.3 bitcast_dynamic-update-slice_fusion.2
  708.0 2.3 bitcast_dynamic-update-slice_fusion.2
  710.9 2.3 bitcast_dynamic-update-slice_fusion.2
  713.8 2.3 bitcast_dynamic-update-slice_fusion.2
  716.7 2.3 bitcast_dynamic-update-slice_fusion.2
  719.6 2.3 bitcast_dynamic-update-slice_fusion.2
  722.5 2.2 bitcast_dynamic-update-slice_fusion.2
  724.7 79.0 %custom-call.70 = f32[8,128,128]{1,2,0:T(8,128)S(1)} custom-call(f32[8,128,128]{2,1,0:T(8,128)S(1)} %get-tuple-element.9), custom_call_target="InvertDiagBlocksLowerTriangular" | custom-call | tf_op jit(solution)/shard_map/jit(_solve_triangular)/triangular_solve | solution.py:72
  803.7 1.9 constant_dynamic-update-slice_fusion.17
  810.4 2.0 fusion.42
  813.2 2.2 fusion.45
  816.2 2.6 convolution_subtract_fusion.2
  819.5 2.8 convolution_subtract_fusion.1
  822.9 3.4 convolution_subtract_fusion.3
  828.9 4.1 copy.40
  833.0 4.1 reshape.95
  (82 shorter events, 44.7 us)
Async XLA Ops:
  7.2 30.0 %copy-start = (bf16[1,1024,4,256]{3,2,1,0:T(4,128)(2,1)S(1)}, bf16[1,1024,4,256]{3,2,1,0:T(4,128)(2,1)}, u32[]{:S(2)}) copy-start(bf16[1,1024,4,256]{3,2,1,0:T(4,128)(2,1)} %param.10) | copy-start | bytes 6291460
  7.2 107.8 %all-gather.5.cloned.1.call-start = ((), (), s32[]{:S(2)}) async-start(), calls=%async_computation.1 | async-start | bytes 10485760 | tf_op jit(solution)/shard_map/all_gather | solution.py:42
  7.9 231.3 %all-gather.7.cloned.1.call-start = ((), (), s32[]{:S(2)}) async-start(), calls=%async_computation.2 | async-start | bytes 15728640 | tf_op jit(solution)/shard_map/all_gather | solution.py:54
  8.7 28.5 %collective-permute-start.1 = (bf16[1024,1024]{1,0:T(8,128)(2,1)}, bf16[1024,1024]{1,0:T(8,128)(2,1)S(1)}, u32[]{:S(2)}, u32[]{:S(2)}) collective-permute-start(bf16[1024,1024]{1,0:T(8,128)(2,1)} %bitcast.188), channel_id=1, source_target_pairs={{28,0},{0,4},{4,8},{8,12},{12,16},{16,20},{20,24},{24,28},{29,1},{... | collective-permute-start | bytes 6291464 | tf_op jit(solution)/shard_map/ppermute | solution.py:34
  9.2 119.9 %collective-permute-start = (bf16[256,6,1024]{2,0,1:T(8,128)(2,1)}, bf16[256,6,1024]{2,0,1:T(8,128)(2,1)}, u32[]{:S(2)}, u32[]{:S(2)}) collective-permute-start(bf16[256,6,1024]{2,0,1:T(8,128)(2,1)} %bitcast.187), channel_id=1, source_target_pairs={{28,0},{0,4},{4,8},{8,12},{12,16},{16,20},{20,24},{24,28},{29,1},{... | collective-permute-start | bytes 9437192 | tf_op jit(solution)/shard_map/ppermute | solution.py:34
  129.1 21.9 %copy-start.5 = (bf16[1,6,6,4,4]{2,4,3,1,0:T(4,128)(2,1)S(1)}, bf16[1,6,6,4,4]{2,4,3,1,0:T(4,128)(2,1)}, u32[]{:S(2)}) copy-start(bf16[1,6,6,4,4]{2,4,3,1,0:T(4,128)(2,1)} %param.11) | copy-start | bytes 3460
  271.7 14.8 %copy-start.4 = (f32[256,4,1024]{2,0,1:T(8,128)}, f32[256,4,1024]{2,0,1:T(8,128)S(1)}, u32[]{:S(2)}) copy-start(f32[256,4,1024]{2,0,1:T(8,128)S(1)} %fusion.10) | copy-start | bytes 12582916
  286.5 92.2 %collective-permute-start.2 = (f32[1024,1024]{0,1:T(8,128)S(1)}, f32[1024,1024]{0,1:T(8,128)S(1)}, u32[]{:S(2)}, u32[]{:S(2)}) collective-permute-start(f32[1024,1024]{0,1:T(8,128)S(1)} %convolution_bitcast_fusion.1), channel_id=1, source_target_pairs={{0,1},{1,0},{2,3},{3,2},{4,5},{5,4},{6,7},{7,6},{8,9},{9,8},{10,11... | collective-permute-start | bytes 12582920 | tf_op jit(solution)/shard_map/ppermute | solution.py:19
  381.7 91.6 %collective-permute-start.3 = (f32[1024,1024]{0,1:T(8,128)}, f32[1024,1024]{0,1:T(8,128)}, u32[]{:S(2)}, u32[]{:S(2)}) collective-permute-start(f32[1024,1024]{0,1:T(8,128)} %add.86), channel_id=1, source_target_pairs={{0,2},{1,3},{2,0},{3,1},{4,6},{5,7},{6,4},{7,5},{8,10},{9,11},{10,... | collective-permute-start | bytes 12582920 | tf_op jit(solution)/shard_map/ppermute | solution.py:19
  490.0 2.0 copy-start.3
  803.7 4.3 copy-start.2
  828.9 10.8 %copy-start.1 = (bf16[1,1024,4,256]{3,2,1,0:T(4,128)(2,1)S(1)}, bf16[1,1024,4,256]{3,2,1,0:T(4,128)(2,1)}, u32[]{:S(2)}) copy-start(bf16[1,1024,4,256]{3,2,1,0:T(4,128)(2,1)} %param.10) | copy-start | bytes 6291460
Sparse Core Ops, SparseCore 0:
  9.8 105.0 all-gather.4
  116.8 122.3 all-gather.6
